TPU v7x, 32 devices: a whole 2x2x4 slice. The times are simulated.
32 devices in a mesh: dp: 4 (over x, core), fsdp: 2 (over y), enc: 4 (over z).
Axes of the slice: x: 2, y: 2, z: 4, core: 2. Of those that a mesh axis runs over, the one named last changes fastest.
Arguments:
- hidden: bfloat16 [8192, 8192], P(('dp', 'fsdp', 'enc')), may hold values from -40 to 40
- residual_gradient: bfloat16 [8192, 8192], P(('dp', 'fsdp', 'enc')), may hold values from -3 to 3
- value_output_gradient: bfloat16 [8192, 1024], P(('dp', 'fsdp', 'enc')), may hold values from -6 to 6
- attention_norm_gain: float32 [8192], replicated, may hold values from 0.1 to 1.9
- value_frozen_weight: bfloat16 [8192, 1024], P('fsdp'), may hold values from -0.0625 to 0.0625
- value_down_factor: bfloat16 [8192, 16], replicated, may hold values from -0.0625 to 0.0625
- value_up_factor: bfloat16 [16, 1024], replicated, may hold values from -0.29882812 to 0.29882812
- merger_frozen_weight: bfloat16 [5120, 8192], P(None, ('fsdp', 'enc')), may hold values from -0.078125 to 0.078125
- merger_down_factor: bfloat16 [5120, 16], replicated, may hold values from -0.078125 to 0.078125
- merger_up_factor: bfloat16 [16, 8192], P(None, ('fsdp', 'enc')), may hold values from -0.29882812 to 0.29882812
- merger_saved_preactivation: bfloat16 [1024, 5120], P(('dp', 'fsdp', 'enc')), may hold values from -5 to 5
- image_token_counts: int32 [32], P('dp'), may hold values from 8 to 16, as said below
- image_encoder_owner: int32 [32], P('dp'), may hold values from 0 to 7, as said below
- image_first_rows: int32 [32], P(('dp', 'fsdp', 'enc')), may hold values from 0 to 255, as said below
Outputs:
- layer_input_gradient: bfloat16 [8192, 8192], P(('dp', 'fsdp', 'enc'))
- preactivation_gradient: bfloat16 [1024, 5120], P(('dp', 'fsdp', 'enc'))
- value_down_gradient: float32 [8192, 16], replicated
- value_up_gradient: float32 [16, 1024], replicated
- merger_down_gradient: float32 [5120, 16], replicated
- merger_up_gradient: float32 [16, 8192], P(None, ('fsdp', 'enc'))
Inputs may be any that keep to these rules, and one draw needn't show every extreme that they name: `image_token_counts`: within each data replica some encoder device owns exactly 2 images, all of 16 visual tokens, so its rows fill all 32; no other device owns more than 2 images. `image_encoder_owner`: encoder devices are numbered within the data replica in mesh order. `image_first_rows`: images of one device lie inside its 256 rows in increasing order and don't intersect.
All inputs are finite; a program needn't handle non-finite values.
Results may differ from a plain program's by a relative error of at most 0.0085.
Values may be sent and summed in bfloat16 or wider, within the bound.
No kernel may reach another device: no remote copies, remote signals or barrier semaphores. Data moves between devices by JAX's collectives and lax.ppermute only.
A program may use at most 192 MiB of HBM per device.

v0:
```python
import jax
import jax.numpy as jnp
from jax import lax
from jax.sharding import PartitionSpec as P

MAXIMG = 16
adapter_scale = 2.0
norm_eps = 1e-06


def gelu_parts(preact):
    normal_cdf = 0.5 * (1.0 + lax.erf(preact * 0.7071067811865476))
    normal_pdf = jnp.exp(-0.5 * preact * preact) * 0.3989422804014327
    return (normal_cdf, normal_pdf)


def owner_layout(image_token_counts, image_encoder_owner, owner_count, owner_room, slot_len):
    total_images = image_token_counts.shape[0]
    image_ids = jnp.arange(total_images)
    same_owner = image_encoder_owner[:, None] == image_encoder_owner[None, :]
    earlier = image_ids[None, :] < image_ids[:, None]
    starts = jnp.sum(jnp.where(same_owner & earlier, image_token_counts[None, :], 0), axis=1)
    row_index = jnp.arange(owner_count * owner_room)
    row_owner = row_index // owner_room
    row_place = row_index % owner_room
    matches = (
        (row_owner[:, None] == image_encoder_owner[None, :])
        & (row_place[:, None] >= starts[None, :])
        & (row_place[:, None] < (starts + image_token_counts)[None, :])
    )
    source = jnp.sum(
        jnp.where(matches, image_ids[None, :] * slot_len + row_place[:, None] - starts[None, :], 0),
        axis=1,
    )
    valid_rows = jnp.any(matches, axis=1)
    return (source, valid_rows)


def take_slots(layer_input_gradient, counts_in, offsets_in):
    padded = jnp.concatenate(
        [
            layer_input_gradient,
            jnp.zeros((MAXIMG, layer_input_gradient.shape[1]), layer_input_gradient.dtype),
        ],
        axis=0,
    )
    window = lax.dynamic_slice_in_dim(padded, offsets_in[0], MAXIMG, 0)
    inside = jnp.arange(MAXIMG) < counts_in[0]
    pieces = jnp.where(inside[:, None], window, jnp.zeros_like(window))
    return pieces


def decoder_layer_block(
    incoming_rows,
    residual_input,
    value_incoming,
    attention_norm_gain,
    passed_gradient,
    value_down_factor,
    value_up_factor,
):
    values = incoming_rows.astype(jnp.float32)
    inverse = lax.rsqrt(jnp.mean(values * values, axis=1, keepdims=True) + norm_eps)
    normalized_input = (values * inverse * attention_norm_gain).astype(jnp.bfloat16)
    value_low_product = jnp.dot(
        value_incoming, value_up_factor.T, preferred_element_type=jnp.float32
    ).astype(jnp.bfloat16)
    normalized_gradient = passed_gradient.astype(jnp.float32) + adapter_scale * jnp.dot(
        value_low_product, value_down_factor.T, preferred_element_type=jnp.float32
    )
    gained = attention_norm_gain * normalized_gradient
    layer_input_gradient = (
        residual_input.astype(jnp.float32)
        + inverse * gained
        - values * inverse**3 * jnp.mean(values * gained, axis=1, keepdims=True)
    ).astype(jnp.bfloat16)
    projected_rows = jnp.dot(
        normalized_input, value_down_factor, preferred_element_type=jnp.float32
    ).astype(jnp.bfloat16)
    up_term = lax.dot_general(
        projected_rows, value_incoming, (((0,), (0,)), ((), ())), preferred_element_type=jnp.float32
    )
    down_term = lax.dot_general(
        normalized_input,
        value_low_product,
        (((0,), (0,)), ((), ())),
        preferred_element_type=jnp.float32,
    )
    return (layer_input_gradient, down_term, up_term)


def body(
    hidden,
    residual_gradient,
    value_output_gradient,
    attention_norm_gain,
    value_frozen_weight,
    value_down_factor,
    value_up_factor,
    merger_frozen_weight,
    merger_down_factor,
    merger_up_factor,
    merger_saved_preactivation,
    image_token_counts,
    image_encoder_owner,
    image_first_rows,
):
    device_total = lax.axis_size("dp") * lax.axis_size("fsdp") * lax.axis_size("enc")
    gradient_scale = 256.0 / (hidden.shape[0] * device_total)
    scale_factor = gradient_scale * adapter_scale
    owner_count = lax.axis_size("fsdp") * lax.axis_size("enc")
    owner_room = merger_saved_preactivation.shape[0]
    preact = merger_saved_preactivation.astype(jnp.float32)
    normal_cdf, normal_pdf = gelu_parts(preact)
    activation = (preact * normal_cdf).astype(jnp.bfloat16)
    act_low = jnp.dot(activation, merger_down_factor, preferred_element_type=jnp.float32).astype(
        jnp.bfloat16
    )
    all_low = lax.all_gather(act_low, ("fsdp", "enc"), axis=0, tiled=True)
    columns = lax.dot_general(
        lax.all_gather(value_output_gradient, "fsdp", axis=0, tiled=True),
        value_frozen_weight,
        (((1,), (1,)), ((), ())),
        preferred_element_type=jnp.float32,
    ).astype(jnp.bfloat16)
    passed_gradient = lax.all_to_all(columns, "fsdp", split_axis=0, concat_axis=1, tiled=True)
    layer_input_gradient, down_term, up_term = decoder_layer_block(
        hidden,
        residual_gradient,
        value_output_gradient,
        attention_norm_gain,
        passed_gradient,
        value_down_factor,
        value_up_factor,
    )
    member = lax.axis_index(("fsdp", "enc"))
    local_images = image_first_rows.shape[0]
    local_counts = lax.dynamic_slice_in_dim(
        image_token_counts, member * local_images, local_images, 0
    )
    slots_out = take_slots(layer_input_gradient, local_counts, image_first_rows)
    received = lax.all_to_all(slots_out, ("fsdp", "enc"), split_axis=1, concat_axis=0, tiled=True)
    source, valid_rows = owner_layout(
        image_token_counts, image_encoder_owner, owner_count, owner_room, MAXIMG
    )
    visual_tokens = jnp.where(
        valid_rows[:, None], jnp.take(received, source, axis=0), jnp.zeros((), received.dtype)
    )
    value_partial_sum = lax.dot_general(
        visual_tokens,
        merger_frozen_weight,
        (((1,), (1,)), ((), ())),
        preferred_element_type=jnp.float32,
    )
    low_part = lax.dot_general(
        visual_tokens,
        merger_up_factor,
        (((1,), (1,)), ((), ())),
        preferred_element_type=jnp.float32,
    )
    value_partial_sum = value_partial_sum + adapter_scale * jnp.dot(
        low_part, merger_down_factor.astype(jnp.float32).T, precision=lax.Precision.HIGHEST
    )
    combined_gradient, low_sum = (
        lax.psum_scatter(value_partial_sum, ("fsdp", "enc"), scatter_dimension=0, tiled=True),
        lax.psum_scatter(low_part, ("fsdp", "enc"), scatter_dimension=0, tiled=True),
    )
    preactivation_gradient = (combined_gradient * (normal_cdf + preact * normal_pdf)).astype(
        jnp.bfloat16
    )
    term_a2 = lax.dot_general(
        activation,
        low_sum.astype(jnp.bfloat16),
        (((0,), (0,)), ((), ())),
        preferred_element_type=jnp.float32,
    )
    term_b2 = lax.dot_general(
        all_low, visual_tokens, (((0,), (0,)), ((), ())), preferred_element_type=jnp.float32
    )
    merger_up_gradient = lax.psum(scale_factor * term_b2, "dp")
    value_down_gradient, value_up_gradient, merger_down_gradient = lax.psum(
        (scale_factor * down_term, scale_factor * up_term, scale_factor * term_a2),
        ("dp", "fsdp", "enc"),
    )
    return (
        layer_input_gradient,
        preactivation_gradient,
        value_down_gradient,
        value_up_gradient,
        merger_down_gradient,
        merger_up_gradient,
    )


def solution(mesh):
    placed = (
        P(("dp", "fsdp", "enc"), None),
        P(("dp", "fsdp", "enc"), None),
        P(("dp", "fsdp", "enc"), None),
        P(),
        P("fsdp", None),
        P(),
        P(),
        P(None, ("fsdp", "enc")),
        P(),
        P(None, ("fsdp", "enc")),
        P(("dp", "fsdp", "enc"), None),
        P("dp"),
        P("dp"),
        P(("dp", "fsdp", "enc")),
    )
    return jax.shard_map(
        body,
        mesh=mesh,
        in_specs=placed,
        out_specs=(
            P(("dp", "fsdp", "enc"), None),
            P(("dp", "fsdp", "enc"), None),
            P(),
            P(),
            P(),
            P(None, ("fsdp", "enc")),
        ),
        check_vma=False,
    )
```

profile of v0, /device:TPU:0, one launch (start us, length us, event | category | flops | bytes accessed | tf_op | source)
XLA Modules:
  0.0 520.8 jit_solution(2232127266080886779)
XLA Ops:
  7.2 0.0 copy-start
  7.2 0.0 all-gather.3.cloned.1.call-start
  7.2 0.7 all-gather.3.cloned.1.call-update
  7.9 25.7 %all-gather.3.cloned.1.call-done = bf16[512,1024]{1,0:T(8,128)(2,1)} async-done(((bf16[256,1024]{1,0:T(8,128)(2,1)}), bf16[512,1024]{1,0:T(8,128)(2,1)}) %all-gather.3.cloned.1.call-update) | async-done | bytes 1048592 | tf_op jit(solution)/shard_map/all_gather | solution.py:121
  33.6 10.3 %convolution_convert_fusion = bf16[512,4096]{1,0:T(8,128)(2,1)} fusion(bf16[512,1024]{1,0:T(8,128)(2,1)} %all-gather.3.cloned.1.call-done, bf16[4096,1024]{1,0:T(8,128)(2,1)} %param.18), kind=kOutput, calls=%fused_computation.19 | convolution fusion | flops 4297064448 | bytes 13631488 | tf_op jit(solution)/shard_map/dot_general | solution.py:120
  43.9 5.7 %all-to-all-start = ((bf16[2,256,4096]{2,1,0:T(8,128)(2,1)}), bf16[2,256,4096]{2,1,0:T(8,128)(2,1)}, u32[]{:S(2)}, u32[]{:S(2)}) async-start(bf16[2,256,4096]{2,1,0:T(8,128)(2,1)} %bitcast.45), calls=%async_computation | async-start | bytes 8388608 | tf_op jit(solution)/shard_map/all_to_all | solution.py:126
  50.3 0.0 copy-done.11
  50.3 0.6 dynamic_slice.6
  50.9 0.0 copy-done.10
  50.9 0.2 select_reduce_fusion.1
  51.1 0.7 iota_compare_fusion.1
  51.7 0.1 select_reduce_fusion
  51.8 0.0 copy-done.5
  51.8 0.0 copy-done.8
  51.9 0.2 convolution_convert_fusion.1
  52.1 45.0 %all-to-all-done = bf16[2,256,4096]{2,1,0:T(8,128)(2,1)} async-done(((bf16[2,256,4096]{2,1,0:T(8,128)(2,1)}), bf16[2,256,4096]{2,1,0:T(8,128)(2,1)}, u32[]{:S(2)}, u32[]{:S(2)}) %all-to-all-start) | async-done | bytes 4194336 | tf_op jit(solution)/shard_map/all_to_all | solution.py:126
  97.1 3.3 convert_bitcast_fusion
  100.4 0.0 copy-start.1
  100.4 0.0 copy-start.7
  100.4 1.0 copy.34
  101.4 1.2 copy-done.1
  102.6 0.0 copy-done.7
  102.6 2.9 fusion.2
  105.5 3.5 fusion.5
  109.0 0.0 copy-start.2
  109.0 2.0 copy-done.2
  111.0 0.1 fusion.28
  111.2 0.7 copy.36
  111.9 4.6 all-to-all-start.1
  116.5 0.2 reduce-scatter.7.cloned.1.call-start
  116.7 0.1 fusion.33
  116.8 8.6 %all-to-all-done.1 = bf16[16,8,1024]{2,0,1:T(8,128)(2,1)S(1)} async-done(((bf16[16,8,1024]{2,0,1:T(8,128)(2,1)}), bf16[16,8,1024]{2,0,1:T(8,128)(2,1)S(1)}, u32[]{:S(2)}, u32[]{:S(2)}) %all-to-all-start.1) | async-done | bytes 262176 | tf_op jit(solution)/shard_map/all_to_all | solution.py:142
  125.4 1.2 gather_fusion
  126.6 0.1 select_select_fusion
  126.8 0.2 fusion.38
  127.0 12.6 %fusion.37 = f32[256,5120]{1,0:T(8,128)} fusion(bf16[256,1024]{1,0:T(8,128)(2,1)S(1)} %select_select_fusion, bf16[5120,1024]{1,0:T(8,128)(2,1)} %param.21), kind=kOutput, calls=%fused_computation.69 | convolution fusion | flops 2684354560 | bytes 16252928 | tf_op jit(solution)/shard_map/dot_general | solution.py:149
  139.6 0.8 copy.31
  140.4 0.0 reduce-scatter.7.cloned.1.call-update
  140.4 0.0 reduce-scatter.5.cloned.1.call-start
  140.5 7.2 %fusion.9 = f32[256,5120]{1,0:T(8,128)} fusion(f32[256,5120]{1,0:T(8,128)} %fusion.37, f32[256,16]{0,1:T(8,128)S(1)} %fusion.38, bf16[5120,16]{0,1:T(8,128)(2,1)S(1)} %copy-done.6), kind=kOutput, calls=%fused_computation.18 | convolution fusion | flops 254279680 | bytes 10665984 | tf_op jit(solution)/shard_map/dot_general | solution.py:161
  147.6 0.0 reduce-scatter.5.cloned.1.call-update
  147.7 0.0 copy-start.4
  147.7 0.0 all-reduce.5.cloned.1.call-start
  147.7 4.2 convolution_multiply_fusion.1
  151.9 4.4 convolution_multiply_fusion.5
  156.3 43.3 %reduce-scatter.7.cloned.1.call-done = f32[32,16]{1,0:T(8,128)} async-done(((f32[256,16]{1,0:T(8,128)}), f32[32,16]{1,0:T(8,128)}) %reduce-scatter.7.cloned.1.call-update) | async-done | bytes 2064
  199.6 0.8 copy.32
  200.4 104.9 %reduce-scatter.5.cloned.1.call-done = f32[32,5120]{1,0:T(8,128)} async-done(((f32[256,5120]{1,0:T(8,128)}), f32[32,5120]{1,0:T(8,128)}) %reduce-scatter.5.cloned.1.call-update) | async-done | bytes 655376 | tf_op jit(solution)/shard_map/reduce_scatter | solution.py:165
  305.3 0.0 copy-done.4
  305.3 2.1 fusion.26
  307.4 0.2 fusion.18
  307.6 30.6 %all-gather = bf16[8,32,16]{1,2,0:T(8,128)(2,1)S(1)} all-gather(bf16[1,32,16]{1,2,0:T(8,128)(2,1)S(1)} %fusion.18), channel_id=1, replica_groups=mesh['dp'=4,'fsdp'=2,'enc'=4] {'fsdp','enc'}, dimensions={0}, use_global_device_ids=true | all-gather | bytes 9216 | tf_op jit(solution)/shard_map/all_gather | solution.py:119
  338.2 0.1 reshape.104
  338.3 0.8 convolution_multiply_fusion.4
  339.1 0.0 all-reduce.5.cloned.1.call-update
  339.2 0.0 all-reduce.7.cloned.1.call-start
  339.2 0.9 convolution_multiply_fusion.3
  340.1 0.0 all-reduce.7.cloned.1.call-update
  340.2 30.3 %all-reduce.5.cloned.1.call-done = f32[16,1024]{1,0:T(8,128)} async-done(((f32[16,1024]{1,0:T(8,128)}), f32[16,1024]{1,0:T(8,128)}) %all-reduce.5.cloned.1.call-update) | async-done | bytes 65552 | tf_op jit(solution)/shard_map/psum | solution.py:180
  370.5 137.3 %all-reduce.7.cloned.1.call-done = (f32[8192,16]{0,1:T(8,128)}, f32[16,1024]{1,0:T(8,128)}, f32[5120,16]{0,1:T(8,128)}) async-done(((f32[8192,16]{0,1:T(8,128)}, f32[16,1024]{1,0:T(8,128)}, f32[5120,16]{0,1:T(8,128)}), (f32[8192,16]{0,1:T(8,128)}, f32[16,1024]{1,0:T(8,128)}, f32[5120,16]{0,1:T(8,128)})) %all-reduce.7.cloned.1.call-update) | async-done | bytes 917520 | tf_op jit(solution)/shard_map/psum | solution.py:181
  507.7 1.9 copy.42
  509.6 1.5 copy.43
  511.1 1.7 copy.44
  512.8 1.5 copy.45
  (19 shorter events, 0.1 us)
Async XLA Ops:
  7.2 94.2 %copy-start = (bf16[8192,16]{0,1:T(8,128)(2,1)S(1)}, bf16[8192,16]{0,1:T(8,128)(2,1)}, u32[]{:S(2)}) copy-start(bf16[8192,16]{0,1:T(8,128)(2,1)} %param.19) | copy-start | bytes 786436
  7.2 26.4 %all-gather.3.cloned.1.call-start = ((), (), s32[]{:S(2)}) async-start(), calls=%async_computation.4 | async-start | bytes 1572864 | tf_op jit(solution)/shard_map/all_gather | solution.py:121
  43.8 6.4 %copy-start.11 = (s32[8]{0:T(128)S(1)}, s32[8]{0:T(128)}, u32[]{:S(2)}) copy-start(s32[8]{0:T(128)} %param.25) | copy-start | bytes 100
  43.9 7.0 %copy-start.10 = (s32[8]{0:T(128)S(1)}, s32[8]{0:T(128)}, u32[]{:S(2)}) copy-start(s32[8]{0:T(128)} %param.26) | copy-start | bytes 100
  43.9 8.0 %copy-start.5 = (bf16[256,1024]{1,0:T(8,128)(2,1)S(1)}, bf16[256,1024]{1,0:T(8,128)(2,1)}, u32[]{:S(2)}) copy-start(bf16[256,1024]{1,0:T(8,128)(2,1)} %param.16) | copy-start | bytes 1572868
  43.9 8.0 %copy-start.8 = (bf16[16,1024]{1,0:T(8,128)(2,1)S(1)}, bf16[16,1024]{1,0:T(8,128)(2,1)}, u32[]{:S(2)}) copy-start(bf16[16,1024]{1,0:T(8,128)(2,1)} %param.20) | copy-start | bytes 98308
  43.9 53.3 %all-to-all-start = ((bf16[2,256,4096]{2,1,0:T(8,128)(2,1)}), bf16[2,256,4096]{2,1,0:T(8,128)(2,1)}, u32[]{:S(2)}, u32[]{:S(2)}) async-start(bf16[2,256,4096]{2,1,0:T(8,128)(2,1)} %bitcast.45), calls=%async_computation | async-start | bytes 8388608 | tf_op jit(solution)/shard_map/all_to_all | solution.py:126
  100.4 2.2 copy-start.1
  100.4 2.2 copy-start.7
  102.6 2.9 copy-start.3
  109.0 2.0 copy-start.2
  111.0 15.7 %copy-start.9 = (bf16[16,1024]{1,0:T(8,128)(2,1)S(1)}, bf16[16,1024]{1,0:T(8,128)(2,1)}, u32[]{:S(2)}) copy-start(bf16[16,1024]{1,0:T(8,128)(2,1)} %param.23) | copy-start | bytes 98308
  111.9 13.6 %all-to-all-start.1 = ((bf16[16,8,1024]{2,0,1:T(8,128)(2,1)}), bf16[16,8,1024]{2,0,1:T(8,128)(2,1)S(1)}, u32[]{:S(2)}, u32[]{:S(2)}) async-start(bf16[16,8,1024]{2,0,1:T(8,128)(2,1)} %bitcast.39), calls=%async_computation.1 | async-start | bytes 524288 | tf_op jit(solution)/shard_map/all_to_all | solution.py:142
  116.5 83.1 %reduce-scatter.7.cloned.1.call-start = ((), (), s32[]{:S(2)}) async-start(), calls=%async_computation.7 | async-start | bytes 147456
  127.0 13.4 %copy-start.6 = (bf16[5120,16]{0,1:T(8,128)(2,1)S(1)}, bf16[5120,16]{0,1:T(8,128)(2,1)}, u32[]{:S(2)}) copy-start(bf16[5120,16]{0,1:T(8,128)(2,1)} %param.22) | copy-start | bytes 491524
  140.4 164.9 %reduce-scatter.5.cloned.1.call-start = ((), (), s32[]{:S(2)}) async-start(), calls=%async_computation.5 | async-start | bytes 5898240 | tf_op jit(solution)/shard_map/reduce_scatter | solution.py:165
  147.7 157.6 %copy-start.4 = (bf16[32,5120]{1,0:T(8,128)(2,1)S(1)}, bf16[32,5120]{1,0:T(8,128)(2,1)}, u32[]{:S(2)}) copy-start(bf16[32,5120]{1,0:T(8,128)(2,1)} %param.24) | copy-start | bytes 983044
  147.7 222.8 %all-reduce.5.cloned.1.call-start = ((), (), s32[]{:S(2)}) async-start(), calls=%async_computation.6 | async-start | bytes 131072 | tf_op jit(solution)/shard_map/psum | solution.py:180
  339.2 168.6 %all-reduce.7.cloned.1.call-start = ((), (), s32[]{:S(2)}) async-start(), calls=%async_computation.8 | async-start | bytes 1835008 | tf_op jit(solution)/shard_map/psum | solution.py:181
Sparse Core Ops, SparseCore 0:
  9.5 23.9 all-gather.2
  140.5 59.0 reduce-scatter.6
  203.2 102.0 reduce-scatter.4
  339.3 31.1 all-reduce.4
  376.4 131.3 all-reduce.6
where the time goes:
time: 522 us; the launch traced here: 521 us
  waiting for transfers between devices  396 us (76%)
  matrix products  44 us (8%)
  blocking collectives  30.6 us (6%)
  local copies, waits for them, and re-layouts  14.9 us (3%)
  between operations  14.6 us (3%)
  starting transfers between devices  10.7 us (2%)
  other arithmetic  10.2 us (2%)
    psum x1, waiting for transfers between devices, body(): lax.psum((scale_factor * down_term, scale_factor * up_term, scale_factor...  137 us
    reduce_scatter x1, waiting for transfers between devices, body(): lax.psum_scatter(value_partial_sum, ('fsdp', 'enc'), scatter_dimension=0,...  105 us
    all_to_all x1, waiting for transfers between devices, body(): lax.all_to_all(columns, 'fsdp', split_axis=0, concat_axis=1, tiled=True)  45 us
    unnamed x6, waiting for transfers between devices  44.1 us
    all_gather x1, blocking collectives, body(): all_low = lax.all_gather(act_low, ('fsdp', 'enc'), axis=0, tiled=True)  30.6 us
    psum x1, waiting for transfers between devices, body(): merger_up_gradient = lax.psum(scale_factor * term_b2, 'dp')  30.3 us
    all_gather x1, waiting for transfers between devices, body(): lax.all_gather(value_output_gradient, 'fsdp', axis=0, tiled=True)  25.7 us
    dot_general x1, matrix products, body(): lax.dot_general(visual_tokens, merger_frozen_weight, (((1,), (1,)), ((),...  12.6 us
  transfers between devices with their start and end apart: 7, of which 7 were waited for; matrix products, arithmetic and copies ran while one was open for 4% of the time, Pallas kernels for 0%

commit v1 on v0

--- a/solution.py
+++ b/solution.py
@@ -123,7 +123,9 @@
         (((1,), (1,)), ((), ())),
         preferred_element_type=jnp.float32,
     ).astype(jnp.bfloat16)
-    passed_gradient = lax.all_to_all(columns, "fsdp", split_axis=0, concat_axis=1, tiled=True)
+    parts = jnp.split(columns, lax.axis_size("fsdp"), axis=0)
+    incoming = lax.all_to_all(jnp.stack(parts), "fsdp", 0, 0)
+    passed_gradient = jnp.concatenate(incoming, axis=1)
     layer_input_gradient, down_term, up_term = decoder_layer_block(
         hidden,
         residual_gradient,

time: 522 us -> 545 us (1.044)
  local copies, waits for them, and re-layouts: 14.9 us -> 31.9 us
    convert_element_type x1 -> x2, local copies, waits for them, and re-layouts: 0.98 us -> 17.8 us  [decoder_layer_block(): passed_gradient.astype(jnp.float32)]
    convert_element_type x0 -> x1, other arithmetic: none -> 6.49 us  [decoder_layer_block(): passed_gradient.astype(jnp.float32)]
where the time goes in v1:
time: 545 us; the launch traced here: 544 us
  waiting for transfers between devices  396 us (73%)
  matrix products  45.2 us (8%)
  local copies, waits for them, and re-layouts  31.9 us (6%)
  blocking collectives  30.6 us (6%)
  other arithmetic  15.6 us (3%)
  between operations  14.7 us (3%)
  starting transfers between devices  10.6 us (2%)
    psum x1, waiting for transfers between devices, body(): lax.psum((scale_factor * down_term, scale_factor * up_term, scale_factor...  137 us
    reduce_scatter x1, waiting for transfers between devices, body(): lax.psum_scatter(value_partial_sum, ('fsdp', 'enc'), scatter_dimension=0,...  105 us
    all_to_all x1, waiting for transfers between devices, body(): incoming = lax.all_to_all(jnp.stack(parts), 'fsdp', 0, 0)  45 us
    unnamed x6, waiting for transfers between devices  44.1 us
    all_gather x1, blocking collectives, body(): all_low = lax.all_gather(act_low, ('fsdp', 'enc'), axis=0, tiled=True)  30.6 us
    psum x1, waiting for transfers between devices, body(): merger_up_gradient = lax.psum(scale_factor * term_b2, 'dp')  30.3 us
    all_gather x1, waiting for transfers between devices, body(): lax.all_gather(value_output_gradient, 'fsdp', axis=0, tiled=True)  25.7 us
    convert_element_type x2, local copies, waits for them, and re-layouts, decoder_layer_block(): passed_gradient.astype(jnp.float32)  17.8 us
  transfers between devices with their start and end apart: 7, of which 7 were waited for; matrix products, arithmetic and copies ran while one was open for 4% of the time, Pallas kernels for 0%

profile of v1, /device:TPU:0, one launch (start us, length us, event | category | flops | bytes accessed | tf_op | source)
XLA Modules:
  0.0 544.4 jit_solution(10508949690327402606)
XLA Ops:
  7.2 0.0 copy-start
  7.2 0.0 all-gather.3.cloned.1.call-start
  7.2 0.7 all-gather.3.cloned.1.call-update
  7.9 25.7 %all-gather.3.cloned.1.call-done = bf16[512,1024]{1,0:T(8,128)(2,1)} async-done(((bf16[256,1024]{1,0:T(8,128)(2,1)}), bf16[512,1024]{1,0:T(8,128)(2,1)}) %all-gather.3.cloned.1.call-update) | async-done | bytes 1048592 | tf_op jit(solution)/shard_map/all_gather | solution.py:121
  33.6 8.3 %convolution_convert_fusion = bf16[512,4096]{1,0:T(8,128)(2,1)S(1)} fusion(bf16[512,1024]{1,0:T(8,128)(2,1)} %all-gather.3.cloned.1.call-done, bf16[4096,1024]{1,0:T(8,128)(2,1)} %param.18), kind=kOutput, calls=%fused_computation.19 | convolution fusion | flops 4297064448 | bytes 13631488 | tf_op jit(solution)/shard_map/dot_general | solution.py:120
  41.8 0.5 slice_bitcast_fusion.1
  42.3 0.0 copy-start.11
  42.3 0.0 copy-start.10
  42.4 0.0 copy-start.5
  42.4 0.0 copy-start.8
  42.4 2.4 pad_maximum_fusion
  44.8 5.6 %all-to-all-start = ((bf16[2,256,4096]{2,1,0:T(8,128)(2,1)}), bf16[2,256,4096]{2,1,0:T(8,128)(2,1)}, u32[]{:S(2)}, u32[]{:S(2)}) async-start(bf16[2,256,4096]{2,1,0:T(8,128)(2,1)} %pad_maximum_fusion), calls=%async_computation | async-start | bytes 8388608 | tf_op jit(solution)/shard_map/all_to_all | solution.py:127
  51.1 0.6 dynamic_slice.6
  51.7 0.2 select_reduce_fusion.1
  51.9 0.7 iota_compare_fusion.1
  52.5 0.1 select_reduce_fusion
  52.6 0.2 convolution_convert_fusion.1
  52.9 45.0 %all-to-all-done = bf16[2,256,4096]{2,1,0:T(8,128)(2,1)} async-done(((bf16[2,256,4096]{2,1,0:T(8,128)(2,1)}), bf16[2,256,4096]{2,1,0:T(8,128)(2,1)}, u32[]{:S(2)}, u32[]{:S(2)}) %all-to-all-start) | async-done | bytes 4194336 | tf_op jit(solution)/shard_map/all_to_all | solution.py:127
  97.9 6.5 %convert_bitcast_fusion = f32[256,2,4096]{2,0,1:T(8,128)} fusion(bf16[2,256,4096]{2,1,0:T(8,128)(2,1)} %all-to-all-done), kind=kLoop, calls=%fused_computation.16 | loop fusion | flops 2097152 | bytes 12582912 | tf_op jit(solution)/shard_map/convert_element_type | solution.py:68
  104.4 8.9 %copy.29 = f32[256,2,4096]{0,2,1:T(8,128)} copy(f32[256,2,4096]{2,0,1:T(8,128)} %convert_bitcast_fusion) | data formatting | bytes 16777216 | tf_op jit(solution)/shard_map/convert_element_type | solution.py:68
  113.3 8.9 %copy.30 = f32[256,8192]{1,0:T(8,128)} copy(f32[256,8192]{0,1:T(8,128)} %bitcast.46) | data formatting | bytes 16777216 | tf_op jit(solution)/shard_map/convert_element_type | solution.py:68
  122.2 0.0 copy-start.3
  122.2 6.2 %fusion.2 = (f32[256]{0:T(256)S(1)}, f32[256]{0:T(256)S(1)}, f32[256,8192]{1,0:T(8,128)S(1)}) fusion(bf16[256,8192]{1,0:T(8,128)(2,1)} %param.14, f32[256,8192]{1,0:T(8,128)} %copy.30, bf16[256,16]{0,1:T(8,128)(2,1)S(1)} %convolution_convert_fusion.1, bf16[8192,16]{0,1:T(8,128)(2,1)S(1)} %copy-done, f32[8192]{0:T(1024)S(1)} %copy-done.7), kind=kOutput, calls=%fused_computation.9 | convolution fusion | flops 83885568 | bytes 21276672 | tf_op jit(solution)/shard_map/dot_general | solution.py:68
  128.5 0.9 copy-done.3
  129.3 3.3 fusion.5
  132.7 0.0 copy-start.2
  132.7 2.0 copy-done.2
  134.7 0.1 fusion.28
  134.8 0.7 copy.37
  135.5 4.6 all-to-all-start.1
  140.1 0.2 reduce-scatter.7.cloned.1.call-start
  140.4 0.1 fusion.33
  140.5 8.6 %all-to-all-done.1 = bf16[16,8,1024]{2,0,1:T(8,128)(2,1)S(1)} async-done(((bf16[16,8,1024]{2,0,1:T(8,128)(2,1)}), bf16[16,8,1024]{2,0,1:T(8,128)(2,1)S(1)}, u32[]{:S(2)}, u32[]{:S(2)}) %all-to-all-start.1) | async-done | bytes 262176 | tf_op jit(solution)/shard_map/all_to_all | solution.py:144
  149.1 1.2 gather_fusion
  150.3 0.1 select_select_fusion
  150.4 0.2 fusion.38
  150.7 12.6 %fusion.37 = f32[256,5120]{1,0:T(8,128)} fusion(bf16[256,1024]{1,0:T(8,128)(2,1)S(1)} %select_select_fusion, bf16[5120,1024]{1,0:T(8,128)(2,1)} %param.21), kind=kOutput, calls=%fused_computation.72 | convolution fusion | flops 2684354560 | bytes 16252928 | tf_op jit(solution)/shard_map/dot_general | solution.py:151
  163.3 0.8 copy.33
  164.0 0.0 reduce-scatter.7.cloned.1.call-update
  164.0 0.0 reduce-scatter.5.cloned.1.call-start
  164.1 7.2 %fusion.9 = f32[256,5120]{1,0:T(8,128)} fusion(f32[256,5120]{1,0:T(8,128)} %fusion.37, f32[256,16]{0,1:T(8,128)S(1)} %fusion.38, bf16[5120,16]{0,1:T(8,128)(2,1)S(1)} %copy-done.6), kind=kOutput, calls=%fused_computation.18 | convolution fusion | flops 254279680 | bytes 10665984 | tf_op jit(solution)/shard_map/dot_general | solution.py:163
  171.3 0.0 reduce-scatter.5.cloned.1.call-update
  171.3 0.0 copy-start.4
  171.3 0.0 all-reduce.5.cloned.1.call-start
  171.3 4.2 convolution_multiply_fusion.1
  175.5 4.4 convolution_multiply_fusion.5
  179.9 43.3 %reduce-scatter.7.cloned.1.call-done = f32[32,16]{1,0:T(8,128)} async-done(((f32[256,16]{1,0:T(8,128)}), f32[32,16]{1,0:T(8,128)}) %reduce-scatter.7.cloned.1.call-update) | async-done | bytes 2064
  223.3 0.8 copy.34
  224.1 104.8 %reduce-scatter.5.cloned.1.call-done = f32[32,5120]{1,0:T(8,128)} async-done(((f32[256,5120]{1,0:T(8,128)}), f32[32,5120]{1,0:T(8,128)}) %reduce-scatter.5.cloned.1.call-update) | async-done | bytes 655376 | tf_op jit(solution)/shard_map/reduce_scatter | solution.py:167
  328.9 2.1 fusion.26
  331.0 0.2 fusion.18
  331.2 30.6 %all-gather = bf16[8,32,16]{1,2,0:T(8,128)(2,1)S(1)} all-gather(bf16[1,32,16]{1,2,0:T(8,128)(2,1)S(1)} %fusion.18), channel_id=1, replica_groups=mesh['dp'=4,'fsdp'=2,'enc'=4] {'fsdp','enc'}, dimensions={0}, use_global_device_ids=true | all-gather | bytes 9216 | tf_op jit(solution)/shard_map/all_gather | solution.py:119
  361.9 0.1 reshape.103
  362.0 0.8 convolution_multiply_fusion.4
  362.8 0.0 all-reduce.5.cloned.1.call-update
  362.8 0.0 all-reduce.7.cloned.1.call-start
  362.8 0.9 convolution_multiply_fusion.3
  363.8 0.0 all-reduce.7.cloned.1.call-update
  363.8 30.3 %all-reduce.5.cloned.1.call-done = f32[16,1024]{1,0:T(8,128)} async-done(((f32[16,1024]{1,0:T(8,128)}), f32[16,1024]{1,0:T(8,128)}) %all-reduce.5.cloned.1.call-update) | async-done | bytes 65552 | tf_op jit(solution)/shard_map/psum | solution.py:182
  394.1 137.3 %all-reduce.7.cloned.1.call-done = (f32[8192,16]{0,1:T(8,128)}, f32[16,1024]{1,0:T(8,128)}, f32[5120,16]{0,1:T(8,128)}) async-done(((f32[8192,16]{0,1:T(8,128)}, f32[16,1024]{1,0:T(8,128)}, f32[5120,16]{0,1:T(8,128)}), (f32[8192,16]{0,1:T(8,128)}, f32[16,1024]{1,0:T(8,128)}, f32[5120,16]{0,1:T(8,128)})) %all-reduce.7.cloned.1.call-update) | async-done | bytes 917520 | tf_op jit(solution)/shard_map/psum | solution.py:183
  531.4 1.9 copy.43
  533.3 1.5 copy.44
  534.7 1.7 copy.45
  536.4 1.5 copy.46
  (22 shorter events, 0.1 us)
Async XLA Ops:
  7.2 115.0 %copy-start = (bf16[8192,16]{0,1:T(8,128)(2,1)S(1)}, bf16[8192,16]{0,1:T(8,128)(2,1)}, u32[]{:S(2)}) copy-start(bf16[8192,16]{0,1:T(8,128)(2,1)} %param.19) | copy-start | bytes 786436
  7.2 26.4 %all-gather.3.cloned.1.call-start = ((), (), s32[]{:S(2)}) async-start(), calls=%async_computation.4 | async-start | bytes 1572864 | tf_op jit(solution)/shard_map/all_gather | solution.py:121
  42.3 8.7 %copy-start.11 = (s32[8]{0:T(128)S(1)}, s32[8]{0:T(128)}, u32[]{:S(2)}) copy-start(s32[8]{0:T(128)} %param.25) | copy-start | bytes 100
  42.3 9.3 %copy-start.10 = (s32[8]{0:T(128)S(1)}, s32[8]{0:T(128)}, u32[]{:S(2)}) copy-start(s32[8]{0:T(128)} %param.26) | copy-start | bytes 100
  42.4 10.3 %copy-start.5 = (bf16[256,1024]{1,0:T(8,128)(2,1)S(1)}, bf16[256,1024]{1,0:T(8,128)(2,1)}, u32[]{:S(2)}) copy-start(bf16[256,1024]{1,0:T(8,128)(2,1)} %param.16) | copy-start | bytes 1572868
  42.4 10.3 %copy-start.8 = (bf16[16,1024]{1,0:T(8,128)(2,1)S(1)}, bf16[16,1024]{1,0:T(8,128)(2,1)}, u32[]{:S(2)}) copy-start(bf16[16,1024]{1,0:T(8,128)(2,1)} %param.20) | copy-start | bytes 98308
  44.8 53.1 %all-to-all-start = ((bf16[2,256,4096]{2,1,0:T(8,128)(2,1)}), bf16[2,256,4096]{2,1,0:T(8,128)(2,1)}, u32[]{:S(2)}, u32[]{:S(2)}) async-start(bf16[2,256,4096]{2,1,0:T(8,128)(2,1)} %pad_maximum_fusion), calls=%async_computation | async-start | bytes 8388608 | tf_op jit(solution)/shard_map/all_to_all | solution.py:127
  113.3 8.9 %copy-start.7 = (f32[8192]{0:T(1024)S(1)}, f32[8192]{0:T(1024)}, u32[]{:S(2)}) copy-start(f32[8192]{0:T(1024)} %param.17) | copy-start | bytes 98308
  122.2 6.2 %copy-start.1 = (bf16[256,8192]{1,0:T(8,128)(2,1)S(1)}, bf16[256,8192]{1,0:T(8,128)(2,1)}, u32[]{:S(2)}) copy-start(bf16[256,8192]{1,0:T(8,128)(2,1)} %param.14) | copy-start | bytes 12582916
  122.2 7.1 %copy-start.3 = (bf16[256,8192]{1,0:T(8,128)(2,1)S(1)}, bf16[256,8192]{1,0:T(8,128)(2,1)}, u32[]{:S(2)}) copy-start(bf16[256,8192]{1,0:T(8,128)(2,1)} %param.15) | copy-start | bytes 12582916
  132.7 2.0 copy-start.2
  134.7 15.7 %copy-start.9 = (bf16[16,1024]{1,0:T(8,128)(2,1)S(1)}, bf16[16,1024]{1,0:T(8,128)(2,1)}, u32[]{:S(2)}) copy-start(bf16[16,1024]{1,0:T(8,128)(2,1)} %param.23) | copy-start | bytes 98308
  135.5 13.6 %all-to-all-start.1 = ((bf16[16,8,1024]{2,0,1:T(8,128)(2,1)}), bf16[16,8,1024]{2,0,1:T(8,128)(2,1)S(1)}, u32[]{:S(2)}, u32[]{:S(2)}) async-start(bf16[16,8,1024]{2,0,1:T(8,128)(2,1)} %bitcast.41), calls=%async_computation.1 | async-start | bytes 524288 | tf_op jit(solution)/shard_map/all_to_all | solution.py:144
  140.1 83.1 %reduce-scatter.7.cloned.1.call-start = ((), (), s32[]{:S(2)}) async-start(), calls=%async_computation.7 | async-start | bytes 147456
  150.7 13.4 %copy-start.6 = (bf16[5120,16]{0,1:T(8,128)(2,1)S(1)}, bf16[5120,16]{0,1:T(8,128)(2,1)}, u32[]{:S(2)}) copy-start(bf16[5120,16]{0,1:T(8,128)(2,1)} %param.22) | copy-start | bytes 491524
  164.0 164.9 %reduce-scatter.5.cloned.1.call-start = ((), (), s32[]{:S(2)}) async-start(), calls=%async_computation.5 | async-start | bytes 5898240 | tf_op jit(solution)/shard_map/reduce_scatter | solution.py:167
  171.3 157.6 %copy-start.4 = (bf16[32,5120]{1,0:T(8,128)(2,1)S(1)}, bf16[32,5120]{1,0:T(8,128)(2,1)}, u32[]{:S(2)}) copy-start(bf16[32,5120]{1,0:T(8,128)(2,1)} %param.24) | copy-start | bytes 983044
  171.3 222.8 %all-reduce.5.cloned.1.call-start = ((), (), s32[]{:S(2)}) async-start(), calls=%async_computation.6 | async-start | bytes 131072 | tf_op jit(solution)/shard_map/psum | solution.py:182
  362.8 168.6 %all-reduce.7.cloned.1.call-start = ((), (), s32[]{:S(2)}) async-start(), calls=%async_computation.8 | async-start | bytes 1835008 | tf_op jit(solution)/shard_map/psum | solution.py:183
Sparse Core Ops, SparseCore 0:
  9.5 23.9 all-gather.2
  164.2 59.0 reduce-scatter.6
  226.9 102.0 reduce-scatter.4
  362.9 31.1 all-reduce.4
  400.0 131.3 all-reduce.6
